TPU v7x, 512 devices: a whole 4x4x16 slice. The times are simulated.
512 devices in a mesh: dp: 32 (over z, core), tensor: 16 (over y, x).
Axes of the slice: x: 4, y: 4, z: 16, core: 2. Of those that a mesh axis runs over, the one named last changes fastest.
Arguments:
- features: bfloat16 [40960, 2048], P(('dp', 'tensor')), may hold values from -6 to 6
- w_hidden: bfloat16 [2048, 2048], P(None, 'tensor'), may hold values from -0.125 to 0.125
- w_embed: bfloat16 [2048, 768], P('tensor'), may hold values from -0.125 to 0.125
- members: bfloat16 [32, 2048, 768], P('dp', 'tensor'), may hold values from -6 to 6
- doc_owner: int32 [40960, 1], P('dp'), may hold values from 0 to 31; in each aligned block of 80 rows (0 to 79, 80 to 159, ...) at most 5 rows name the same one
- doc_local: int32 [40960], P('dp'), may hold values from 0 to 15
- member_cluster: int32 [32, 2048], P('dp', 'tensor'), may hold values from 0 to 15, never falling along the last dimension, each value on 1 to 192 neighbouring positions
- member_valid: int32 [32, 2048], P('dp', 'tensor'), may hold values 0 or 1
Outputs:
- best: float32 [40960], P(('dp', 'tensor'))
Inputs may be any that keep to these rules, and one draw needn't show every extreme that they name: Among the 80 documents of one device (aligned blocks of doc_owner's rows, in the order of dp then tensor) no owner is named more than 5 times; some owner is named exactly 5 times. `member_cluster`: along each owner's row the clusters never fall; every cluster has 1 to 192 slots.
All inputs are finite; a program needn't handle non-finite values. No bound on the sum of `member_valid` on one device may be relied on, other than what follows from the above.
Results may differ from a plain program's by a relative error of at most 0.013.
Values may be sent and summed in bfloat16 or wider, within the bound.
No kernel may reach another device: no remote copies, remote signals or barrier semaphores. Data moves between devices by JAX's collectives and lax.ppermute only.
A program may use at most 64 MiB of HBM per device.

v0:
```python
import jax
import jax.numpy as jnp
from jax import lax
from jax.sharding import PartitionSpec as P

epsilon = 1e-06


def unit_rows(vectors):
    values = vectors.astype(jnp.float32)
    return (values / jnp.sqrt(jnp.sum(values * values, axis=-1, keepdims=True) + epsilon)).astype(
        jnp.bfloat16
    )


def slot_of(owner, owners_count, slot_cap):
    onehot = (owner[:, None] == jnp.arange(owners_count, dtype=jnp.int32)[None, :]).astype(
        jnp.int32
    )
    ranking = jnp.sum((jnp.cumsum(onehot, axis=0) - 1) * onehot, axis=1)
    return owner * slot_cap + ranking


def pack_rows(query, local, slot_index, slot_total):
    placing = slot_index[None, :] == jnp.arange(slot_total, dtype=jnp.int32)[:, None]
    outgoing = jnp.dot(
        placing.astype(jnp.bfloat16), query, preferred_element_type=jnp.float32
    ).astype(jnp.bfloat16)
    slot_tag = jnp.sum(jnp.where(placing, local[None, :] + 1, 0), axis=1)
    return (outgoing, slot_tag)


def best_scores(arrived, arrived_tag, unit, cluster_here, valid_here):
    scores = lax.dot_general(
        arrived, unit, (((1,), (1,)), ((), ())), preferred_element_type=jnp.float32
    )
    allowed = (valid_here[None, :] == 1) & (cluster_here[None, :] == arrived_tag[:, None] - 1)
    return jnp.max(jnp.where(allowed, scores, -1.0), axis=1)


def body(features, w_hidden, w_embed, members, doc_owner, doc_local, member_cluster, member_valid):
    owners_count = lax.axis_size("dp")
    tensor_index = lax.axis_index("tensor")
    row_total = features.shape[0]
    slot_cap = min(row_total, max(2, 2 * row_total // owners_count))
    hidden = jax.nn.gelu(
        jnp.dot(
            lax.all_gather(features, "tensor", axis=0, tiled=True),
            w_hidden,
            preferred_element_type=jnp.float32,
        )
    ).astype(jnp.bfloat16)
    unit = unit_rows(members.reshape(members.shape[1], members.shape[2]))
    cluster_here = member_cluster.reshape(-1)
    valid_here = member_valid.reshape(-1)
    owner_all = doc_owner[:, 0]
    summed = lax.psum_scatter(
        jnp.dot(hidden, w_embed, preferred_element_type=jnp.float32).astype(jnp.bfloat16),
        "tensor",
        scatter_dimension=0,
        tiled=True,
    ).astype(jnp.float32)
    query = unit_rows(summed)
    owner = lax.dynamic_slice_in_dim(owner_all, tensor_index * row_total, row_total, 0)
    local = lax.dynamic_slice_in_dim(doc_local, tensor_index * row_total, row_total, 0)
    slot_total = owners_count * slot_cap
    slot_index = slot_of(owner, owners_count, slot_cap)
    outgoing, slot_tag = pack_rows(query, local, slot_index, slot_total)
    arrived, arrived_tag = (
        lax.all_to_all(outgoing, "dp", split_axis=0, concat_axis=0, tiled=True),
        lax.all_to_all(slot_tag, "dp", split_axis=0, concat_axis=0, tiled=True),
    )
    shared, shared_tag = (
        lax.all_gather(arrived, "tensor", axis=0, tiled=True),
        lax.all_gather(arrived_tag, "tensor", axis=0, tiled=True),
    )
    partial_value = best_scores(shared, shared_tag, unit, cluster_here, valid_here)
    merged = lax.pmax(partial_value, "tensor")
    own_best = lax.dynamic_slice_in_dim(merged, tensor_index * slot_total, slot_total, 0)
    answers = lax.all_to_all(own_best, "dp", split_axis=0, concat_axis=0, tiled=True)
    return jnp.take(answers, slot_index, axis=0)


def solution(mesh):
    return jax.shard_map(
        body,
        mesh=mesh,
        in_specs=(
            P(("dp", "tensor"), None),
            P(None, "tensor"),
            P("tensor", None),
            P("dp", "tensor", None),
            P("dp", None),
            P("dp"),
            P("dp", "tensor"),
            P("dp", "tensor"),
        ),
        out_specs=P(("dp", "tensor")),
        check_vma=False,
    )
```

profile of v0, /device:TPU:1, one launch (start us, length us, event | category | flops | bytes accessed | tf_op | source)
XLA Modules:
  0.0 418.8 jit_solution(9117724124348048883)
XLA Ops:
  6.5 0.7 all-gather.3.cloned.1.call-update
  7.3 80.1 %all-gather.3.cloned.1.call-done = bf16[1280,2048]{1,0:T(8,128)(2,1)} async-done(((bf16[80,2048]{1,0:T(8,128)(2,1)}), bf16[1280,2048]{1,0:T(8,128)(2,1)}) %all-gather.3.cloned.1.call-update) | async-done | bytes 5242896 | tf_op jit(solution)/shard_map/all_gather | solution.py:48
  87.4 6.7 %convolution_convert_fusion = bf16[1280,768]{1,0:T(8,128)(2,1)} fusion(bf16[128,768]{1,0:T(8,128)(2,1)} %param.10, bf16[1280,2048]{1,0:T(8,128)(2,1)} %all-gather.3.cloned.1.call-done, bf16[2048,128]{1,0:T(8,128)(2,1)S(1)} %copy-done), kind=kOutput, calls=%fused_computation.2 | convolution fusion | flops 925204480 | bytes 7929856 | tf_op jit(solution)/shard_map/dot_general | solution.py:58
  94.2 0.8 fusion.25
  95.0 0.1 reduce_window_sum.11
  95.1 0.2 select_reduce_fusion.1
  95.3 0.8 multiply_add_fusion
  96.1 85.9 %reduce-scatter.2.cloned.1.call-done = bf16[80,768]{1,0:T(8,128)(2,1)} async-done(((bf16[1280,768]{1,0:T(8,128)(2,1)}), bf16[80,768]{1,0:T(8,128)(2,1)}) %reduce-scatter.2.cloned.1.call-update) | async-done | bytes 122896 | tf_op jit(solution)/shard_map/reduce_scatter | solution.py:57
  182.0 1.0 fusion.16
  183.0 1.2 convolution_convert_fusion.1
  184.3 42.5 %all_to_all.36 = bf16[32,5,768]{2,1,0:T(8,128)(2,1)S(1)} all-to-all(bf16[32,5,768]{2,1,0:T(8,128)(2,1)S(1)} %all_to_all.27), channel_id=1, replica_groups=mesh['dp'=32,'tensor'=16] {'dp'}, dimensions={0} | all-to-all | bytes 491520 | tf_op jit(solution)/shard_map/all_to_all | solution.py:70
  226.8 0.8 all_to_all.29
  227.6 0.8 dynamic-slice_add_fusion
  228.5 0.7 all_to_all.24
  229.3 3.9 all-to-all-start
  233.2 0.1 fusion.9
  233.3 0.8 compare_select_fusion
  234.1 1.3 dynamic-slice.1
  236.0 9.0 %all-to-all-done = s32[32,5,1]{1,2,0:T(1,128)S(1)} async-done(((s32[32,5,1]{1,2,0:T(1,128)}), s32[32,5,1]{1,2,0:T(1,128)S(1)}, u32[]{:S(2)}, u32[]{:S(2)}) %all-to-all-start) | async-done | bytes 672 | tf_op jit(solution)/shard_map/all_to_all | solution.py:71
  245.0 0.5 broadcast.54
  245.5 0.7 reduce.6
  246.3 0.3 dynamic-update-slice
  246.6 58.3 %all-reduce = s32[2560]{0:T(1024)S(1)} all-reduce(s32[2560]{0:T(1024)S(1)} %dynamic-update-slice), channel_id=1, replica_groups=mesh['dp'=32,'tensor'=16] {'tensor'}, use_global_device_ids=true, to_apply=%add | all-reduce | flops 2560 | bytes 20480
  304.9 3.5 fusion
  308.5 55.9 %pmax.7 = f32[2560]{0:T(1024)S(1)} all-reduce(f32[2560]{0:T(1024)S(1)} %fusion), channel_id=1, replica_groups=mesh['dp'=32,'tensor'=16] {'tensor'}, use_global_device_ids=true, to_apply=%region_7.8 | all-reduce | flops 2560 | bytes 20480 | tf_op jit(solution)/shard_map/pmax | solution.py:78
  364.5 0.7 all_to_all.30
  365.2 32.1 %all-to-all-start.2 = ((f32[32,5,1]{1,2,0:T(1,128)}), f32[32,5,1]{1,2,0:T(1,128)S(1)}, u32[]{:S(2)}, u32[]{:S(2)}) async-start(f32[32,5,1]{1,2,0:T(1,128)} %bitcast.9), calls=%async_computation.3 | async-start | bytes 32768 | tf_op jit(solution)/shard_map/all_to_all | solution.py:80
  397.3 11.9 %all-to-all-done.2 = f32[32,5,1]{1,2,0:T(1,128)S(1)} async-done(((f32[32,5,1]{1,2,0:T(1,128)}), f32[32,5,1]{1,2,0:T(1,128)S(1)}, u32[]{:S(2)}, u32[]{:S(2)}) %all-to-all-start.2) | async-done | bytes 672 | tf_op jit(solution)/shard_map/all_to_all | solution.py:80
  409.2 0.5 broadcast.55
  409.7 0.7 reduce.7
  410.5 1.3 gather_fusion
  411.7 0.5 bitcast_select_fusion
  (26 shorter events, 0.7 us)
Async XLA Ops:
  6.5 80.9 %copy-start = (bf16[2048,128]{1,0:T(8,128)(2,1)S(1)}, bf16[2048,128]{1,0:T(8,128)(2,1)}, u32[]{:S(2)}) copy-start(bf16[2048,128]{1,0:T(8,128)(2,1)} %param.9) | copy-start | bytes 1572868
  6.5 80.9 %all-gather.3.cloned.1.call-start = ((), (), s32[]{:S(2)}) async-start(), calls=%async_computation.4 | async-start | bytes 5570560 | tf_op jit(solution)/shard_map/all_gather | solution.py:48
  7.3 174.7 %reduce-scatter.2.cloned.1.call-start = ((), (), s32[]{:S(2)}) async-start(), calls=%async_computation.5 | async-start | bytes 2088960 | tf_op jit(solution)/shard_map/reduce_scatter | solution.py:57
  94.1 139.1 %copy-start.1 = (bf16[1,128,768]{2,1,0:T(8,128)(2,1)S(1)}, bf16[1,128,768]{2,1,0:T(8,128)(2,1)}, u32[]{:S(2)}) copy-start(bf16[1,128,768]{2,1,0:T(8,128)(2,1)} %param.11) | copy-start | bytes 589828
  94.1 140.0 %copy-start.2 = (s32[1,128]{1,0:T(1,128)S(1)}, s32[1,128]{1,0:T(1,128)}, u32[]{:S(2)}) copy-start(s32[1,128]{1,0:T(1,128)} %param.15) | copy-start | bytes 1540
  94.1 210.9 %copy-start.3 = (s32[1,128]{1,0:T(1,128)S(1)}, s32[1,128]{1,0:T(1,128)}, u32[]{:S(2)}) copy-start(s32[1,128]{1,0:T(1,128)} %param.14) | copy-start | bytes 1540
  94.1 210.8 %all-gather.5.cloned.1.call-start = ((), (), s32[]{:S(2)}) async-start(), calls=%async_computation.6 | async-start | bytes 4177920 | tf_op jit(solution)/shard_map/all_gather | solution.py:74
  229.3 15.8 %all-to-all-start = ((s32[32,5,1]{1,2,0:T(1,128)}), s32[32,5,1]{1,2,0:T(1,128)S(1)}, u32[]{:S(2)}, u32[]{:S(2)}) async-start(s32[32,5,1]{1,2,0:T(1,128)} %bitcast.5), calls=%async_computation | async-start | bytes 32768 | tf_op jit(solution)/shard_map/all_to_all | solution.py:71
  365.2 44.0 %all-to-all-start.2 = ((f32[32,5,1]{1,2,0:T(1,128)}), f32[32,5,1]{1,2,0:T(1,128)S(1)}, u32[]{:S(2)}, u32[]{:S(2)}) async-start(f32[32,5,1]{1,2,0:T(1,128)} %bitcast.9), calls=%async_computation.3 | async-start | bytes 32768 | tf_op jit(solution)/shard_map/all_to_all | solution.py:80
Sparse Core Ops, SparseCore 0:
  10.4 76.9 all-gather.2
  94.2 87.7 reduce-scatter.1
  227.8 55.1 all-gather.4
where the time goes:
time: 419 us
  waiting for transfers between devices  188 us (45%)
  blocking collectives  157 us (37%)
  starting transfers between devices  36.1 us (9%)
  between operations  13.9 us (3%)
  matrix products  11.4 us (3%)
  local copies, waits for them, and re-layouts  7.26 us (2%)
  other arithmetic  5.84 us (1%)
    reduce_scatter x1, waiting for transfers between devices, body(): lax.psum_scatter(jnp.dot(hidden, w_embed, preferred_element_type=jnp.floa...  85.9 us
    all_gather x1, waiting for transfers between devices, body(): lax.all_gather(features, 'tensor', axis=0, tiled=True)  80.1 us
    unnamed x1, blocking collectives  58.3 us
    pmax x1, blocking collectives, body(): merged = lax.pmax(partial_value, 'tensor')  55.9 us
    all_to_all x1, blocking collectives, body(): lax.all_to_all(outgoing, 'dp', split_axis=0, concat_axis=0, tiled=True)  42.5 us
    all_to_all x1, starting transfers between devices, body(): lax.all_to_all(own_best, 'dp', split_axis=0, concat_axis=0, tiled=True)  32.1 us
    all_to_all x1, waiting for transfers between devices, body(): lax.all_to_all(own_best, 'dp', split_axis=0, concat_axis=0, tiled=True)  11.9 us
    all_to_all x1, waiting for transfers between devices, body(): lax.all_to_all(slot_tag, 'dp', split_axis=0, concat_axis=0, tiled=True)  8.98 us
  transfers between devices with their start and end apart: 5, of which 4 were waited for; matrix products, arithmetic and copies ran while one was open for 2% of the time, Pallas kernels for 0%

commit v1 on v0

--- a/solution.py
+++ b/solution.py
@@ -43,12 +43,29 @@
     tensor_index = lax.axis_index("tensor")
     row_total = features.shape[0]
     slot_cap = min(row_total, max(2, 2 * row_total // owners_count))
+
+    def _turn_ranges(inputs):
+        z2, spare, last = (lax.axis_size("tensor"), lax.axis_index("tensor"), inputs.shape[0])
+        all_blocks = tuple(((dev, (dev + 1) % z2) for dev in range(z2)))
+        column = tuple(((dev, (dev - 1) % z2) for dev in range(z2)))
+        n_now = jnp.zeros((*inputs.shape[:0], z2 * last, *inputs.shape[1:]), inputs.dtype)
+        n_now = lax.dynamic_update_slice_in_dim(n_now, inputs, spare * last, axis=0)
+        then = right_arr = inputs
+        outer = z2 // 2
+        w = 1
+        while w < outer + 1:
+            then = lax.ppermute(then, "tensor", all_blocks)
+            n_now = lax.dynamic_update_slice_in_dim(n_now, then, (spare - w) % z2 * last, axis=0)
+            if w < z2 - outer:
+                right_arr = lax.ppermute(right_arr, "tensor", column)
+                n_now = lax.dynamic_update_slice_in_dim(
+                    n_now, right_arr, (spare + w) % z2 * last, axis=0
+                )
+            w = w + 1
+        return n_now
+
     hidden = jax.nn.gelu(
-        jnp.dot(
-            lax.all_gather(features, "tensor", axis=0, tiled=True),
-            w_hidden,
-            preferred_element_type=jnp.float32,
-        )
+        jnp.dot(_turn_ranges(features), w_hidden, preferred_element_type=jnp.float32)
     ).astype(jnp.bfloat16)
     unit = unit_rows(members.reshape(members.shape[1], members.shape[2]))
     cluster_here = member_cluster.reshape(-1)

time: 419 us -> 444 us (1.060)
  starting transfers between devices: 36.1 us -> 100 us
  waiting for transfers between devices: 188 us -> 132 us
  local copies, waits for them, and re-layouts: 7.26 us -> 22.2 us
    all_gather x1 -> x0, waiting for transfers between devices: 80.1 us -> none  [body(): lax.all_gather(features, 'tensor', axis=0, tiled=True)]
    ppermute x0 -> x15, starting transfers between devices: none -> 64.3 us  [the longest x7 46.9 us: _turn_ranges(): right_arr = lax.ppermute(right_arr, 'tensor', column)]
    ppermute x0 -> x15, waiting for transfers between devices: none -> 23.4 us  [the longest x8 22.8 us: _turn_ranges(): then = lax.ppermute(then, 'tensor', all_blocks)]
    dynamic_update_slice x0 -> x16, local copies, waits for them, and re-layouts: none -> 12 us  [the longest x8 6.04 us: _turn_ranges(): lax.dynamic_update_slice_in_dim(n_now, then, (spare - w) % z2 * last, axi...]
  transfers between devices with their start and end apart: 5 -> 19, of which waited for: 4 -> 12; matrix products, arithmetic and copies ran while one was open for 2% -> 5% of each run, Pallas kernels for 0% -> 0%
where the time goes in v1:
time: 444 us; the launch traced here: 443 us
  blocking collectives  157 us (35%)
  waiting for transfers between devices  132 us (30%)
  starting transfers between devices  100 us (23%)
  local copies, waits for them, and re-layouts  22.2 us (5%)
  between operations  14.7 us (3%)
  matrix products  11.4 us (3%)
  other arithmetic  5.84 us (1%)
    reduce_scatter x1, waiting for transfers between devices, body(): lax.psum_scatter(jnp.dot(hidden, w_embed, preferred_element_type=jnp.floa...  87.5 us
    unnamed x1, blocking collectives  58.3 us
    pmax x1, blocking collectives, body(): merged = lax.pmax(partial_value, 'tensor')  55.9 us
    ppermute x7, starting transfers between devices, _turn_ranges(): right_arr = lax.ppermute(right_arr, 'tensor', column)  46.9 us
    all_to_all x1, blocking collectives, body(): lax.all_to_all(outgoing, 'dp', split_axis=0, concat_axis=0, tiled=True)  42.5 us
    all_to_all x1, starting transfers between devices, body(): lax.all_to_all(own_best, 'dp', split_axis=0, concat_axis=0, tiled=True)  32.1 us
    ppermute x8, waiting for transfers between devices, _turn_ranges(): then = lax.ppermute(then, 'tensor', all_blocks)  22.8 us
    ppermute x8, starting transfers between devices, _turn_ranges(): then = lax.ppermute(then, 'tensor', all_blocks)  17.4 us
  transfers between devices with their start and end apart: 19, of which 12 were waited for; matrix products, arithmetic and copies ran while one was open for 5% of the time, Pallas kernels for 0%

profile of v1, /device:TPU:1, one launch (start us, length us, event | category | flops | bytes accessed | tf_op | source)
XLA Modules:
  0.0 443.0 jit_solution(2216455451812724818)
XLA Ops:
  6.5 4.1 collective-permute-start
  10.6 5.6 %collective-permute-start.1 = (bf16[80,2048]{1,0:T(8,128)(2,1)}, bf16[80,2048]{1,0:T(8,128)(2,1)S(1)}, u32[]{:S(2)}, u32[]{:S(2)}) collective-permute-start(bf16[80,2048]{1,0:T(8,128)(2,1)} %param.8), channel_id=1, source_target_pairs={{0,15},{1,0},{2,1},{3,2},{4,3},{5,4},{6,5},{7,6},{8,7},{9,8},{10,9... | collective-permute-start | bytes 983048 | tf_op jit(solution)/shard_map/ppermute | solution.py:60
  16.5 3.0 broadcast_in_dim.35
  20.3 1.9 collective-permute-start.2
  22.2 6.7 %collective-permute-start.3 = (bf16[80,2048]{1,0:T(8,128)(2,1)S(1)}, bf16[80,2048]{1,0:T(8,128)(2,1)S(1)}, u32[]{:S(2)}, u32[]{:S(2)}) collective-permute-start(bf16[80,2048]{1,0:T(8,128)(2,1)S(1)} %collective-permute-done.1), channel_id=1, source_target_pairs={{0,15},{1,0},{2,1},{3,2},{4,3},{5,4},{6,5},{7,6},{8,7},{9,8},{10,9... | collective-permute-start | bytes 983048 | tf_op jit(solution)/shard_map/ppermute | solution.py:60
  31.4 1.9 collective-permute-start.4
  33.3 6.7 %collective-permute-start.5 = (bf16[80,2048]{1,0:T(8,128)(2,1)S(1)}, bf16[80,2048]{1,0:T(8,128)(2,1)S(1)}, u32[]{:S(2)}, u32[]{:S(2)}) collective-permute-start(bf16[80,2048]{1,0:T(8,128)(2,1)S(1)} %collective-permute-done.3), channel_id=1, source_target_pairs={{0,15},{1,0},{2,1},{3,2},{4,3},{5,4},{6,5},{7,6},{8,7},{9,8},{10,9... | collective-permute-start | bytes 983048 | tf_op jit(solution)/shard_map/ppermute | solution.py:60
  42.5 1.9 collective-permute-start.6
  44.4 6.7 %collective-permute-start.7 = (bf16[80,2048]{1,0:T(8,128)(2,1)S(1)}, bf16[80,2048]{1,0:T(8,128)(2,1)S(1)}, u32[]{:S(2)}, u32[]{:S(2)}) collective-permute-start(bf16[80,2048]{1,0:T(8,128)(2,1)S(1)} %collective-permute-done.5), channel_id=1, source_target_pairs={{0,15},{1,0},{2,1},{3,2},{4,3},{5,4},{6,5},{7,6},{8,7},{9,8},{10,9... | collective-permute-start | bytes 983048 | tf_op jit(solution)/shard_map/ppermute | solution.py:60
  52.6 1.4 collective-permute-done.6
  54.1 1.9 collective-permute-start.8
  56.0 7.0 %collective-permute-start.9 = (bf16[80,2048]{1,0:T(8,128)(2,1)S(1)}, bf16[80,2048]{1,0:T(8,128)(2,1)S(1)}, u32[]{:S(2)}, u32[]{:S(2)}) collective-permute-start(bf16[80,2048]{1,0:T(8,128)(2,1)S(1)} %collective-permute-done.7), channel_id=1, source_target_pairs={{0,15},{1,0},{2,1},{3,2},{4,3},{5,4},{6,5},{7,6},{8,7},{9,8},{10,9... | collective-permute-start | bytes 983048 | tf_op jit(solution)/shard_map/ppermute | solution.py:60
  64.5 2.2 collective-permute-done.8
  66.7 1.9 collective-permute-start.10
  68.8 7.1 %collective-permute-start.11 = (bf16[80,2048]{1,0:T(8,128)(2,1)S(1)}, bf16[80,2048]{1,0:T(8,128)(2,1)S(1)}, u32[]{:S(2)}, u32[]{:S(2)}) collective-permute-start(bf16[80,2048]{1,0:T(8,128)(2,1)S(1)} %collective-permute-done.9), channel_id=1, source_target_pairs={{0,15},{1,0},{2,1},{3,2},{4,3},{5,4},{6,5},{7,6},{8,7},{9,8},{10,9... | collective-permute-start | bytes 983048 | tf_op jit(solution)/shard_map/ppermute | solution.py:60
  77.4 3.1 collective-permute-done.10
  80.5 1.9 collective-permute-start.12
  82.8 7.1 %collective-permute-start.13 = (bf16[80,2048]{1,0:T(8,128)(2,1)S(1)}, bf16[80,2048]{1,0:T(8,128)(2,1)S(1)}, u32[]{:S(2)}, u32[]{:S(2)}) collective-permute-start(bf16[80,2048]{1,0:T(8,128)(2,1)S(1)} %collective-permute-done.11), channel_id=1, source_target_pairs={{0,15},{1,0},{2,1},{3,2},{4,3},{5,4},{6,5},{7,6},{8,7},{9,8},{10,9... | collective-permute-start | bytes 983048 | tf_op jit(solution)/shard_map/ppermute | solution.py:60
  91.5 3.7 collective-permute-done.12
  95.2 1.9 collective-permute-start.14
  98.6 10.4 %collective-permute-done.14 = bf16[80,2048]{1,0:T(8,128)(2,1)S(1)} collective-permute-done((bf16[80,2048]{1,0:T(8,128)(2,1)S(1)}, bf16[80,2048]{1,0:T(8,128)(2,1)S(1)}, u32[]{:S(2)}, u32[]{:S(2)}) %collective-permute-start.14) | collective-permute-done | bytes 327712 | tf_op jit(solution)/shard_map/ppermute | solution.py:57
  109.7 6.7 %convolution_convert_fusion = bf16[1280,768]{1,0:T(8,128)(2,1)} fusion(bf16[128,768]{1,0:T(8,128)(2,1)S(1)} %copy-done.3, bf16[1280,2048]{1,0:T(8,128)(2,1)} %constant_dynamic-update-slice_fusion, bf16[2048,128]{1,0:T(8,128)(2,1)S(1)} %copy-done), kind=kOutput, calls=%fused_computation.2 | convolution fusion | flops 925204480 | bytes 7929856 | tf_op jit(solution)/shard_map/dot_general | solution.py:75
  118.4 87.5 %reduce-scatter.2.cloned.1.call-done = bf16[80,768]{1,0:T(8,128)(2,1)} async-done(((bf16[1280,768]{1,0:T(8,128)(2,1)}), bf16[80,768]{1,0:T(8,128)(2,1)}) %reduce-scatter.2.cloned.1.call-update) | async-done | bytes 122896 | tf_op jit(solution)/shard_map/reduce_scatter | solution.py:74
  208.3 42.5 %all_to_all.36 = bf16[32,5,768]{2,1,0:T(8,128)(2,1)S(1)} all-to-all(bf16[32,5,768]{2,1,0:T(8,128)(2,1)S(1)} %all_to_all.27), channel_id=1, replica_groups=mesh['dp'=32,'tensor'=16] {'dp'}, dimensions={0} | all-to-all | bytes 491520 | tf_op jit(solution)/shard_map/all_to_all | solution.py:87
  253.2 3.9 all-to-all-start
  258.0 1.3 dynamic-slice.1
  260.0 9.0 %all-to-all-done = s32[32,5,1]{1,2,0:T(1,128)S(1)} async-done(((s32[32,5,1]{1,2,0:T(1,128)}), s32[32,5,1]{1,2,0:T(1,128)S(1)}, u32[]{:S(2)}, u32[]{:S(2)}) %all-to-all-start) | async-done | bytes 672 | tf_op jit(solution)/shard_map/all_to_all | solution.py:88
  270.6 58.3 %all-reduce = s32[2560]{0:T(1024)S(1)} all-reduce(s32[2560]{0:T(1024)S(1)} %dynamic-update-slice), channel_id=1, replica_groups=mesh['dp'=32,'tensor'=16] {'tensor'}, use_global_device_ids=true, to_apply=%add | all-reduce | flops 2560 | bytes 20480
  328.9 3.5 fusion
  332.4 55.9 %pmax.7 = f32[2560]{0:T(1024)S(1)} all-reduce(f32[2560]{0:T(1024)S(1)} %fusion), channel_id=1, replica_groups=mesh['dp'=32,'tensor'=16] {'tensor'}, use_global_device_ids=true, to_apply=%region_7.8 | all-reduce | flops 2560 | bytes 20480 | tf_op jit(solution)/shard_map/pmax | solution.py:95
  389.1 32.1 %all-to-all-start.2 = ((f32[32,5,1]{1,2,0:T(1,128)}), f32[32,5,1]{1,2,0:T(1,128)S(1)}, u32[]{:S(2)}, u32[]{:S(2)}) async-start(f32[32,5,1]{1,2,0:T(1,128)} %bitcast.9), calls=%async_computation.3 | async-start | bytes 32768 | tf_op jit(solution)/shard_map/all_to_all | solution.py:97
  421.2 11.9 %all-to-all-done.2 = f32[32,5,1]{1,2,0:T(1,128)S(1)} async-done(((f32[32,5,1]{1,2,0:T(1,128)}), f32[32,5,1]{1,2,0:T(1,128)S(1)}, u32[]{:S(2)}, u32[]{:S(2)}) %all-to-all-start.2) | async-done | bytes 672 | tf_op jit(solution)/shard_map/all_to_all | solution.py:97
  (74 shorter events, 27.7 us)
Async XLA Ops:
  6.5 103.2 %copy-start = (bf16[2048,128]{1,0:T(8,128)(2,1)S(1)}, bf16[2048,128]{1,0:T(8,128)(2,1)}, u32[]{:S(2)}) copy-start(bf16[2048,128]{1,0:T(8,128)(2,1)} %param.9) | copy-start | bytes 1572868
  6.5 13.0 %copy-start.1 = (bf16[80,2048]{1,0:T(8,128)(2,1)S(1)}, bf16[80,2048]{1,0:T(8,128)(2,1)}, u32[]{:S(2)}) copy-start(bf16[80,2048]{1,0:T(8,128)(2,1)} %param.8) | copy-start | bytes 983044
  6.5 199.4 %reduce-scatter.2.cloned.1.call-start = ((), (), s32[]{:S(2)}) async-start(), calls=%async_computation.4 | async-start | bytes 2088960 | tf_op jit(solution)/shard_map/reduce_scatter | solution.py:74
  6.5 13.7 %collective-permute-start = (bf16[80,2048]{1,0:T(8,128)(2,1)}, bf16[80,2048]{1,0:T(8,128)(2,1)S(1)}, u32[]{:S(2)}, u32[]{:S(2)}) collective-permute-start(bf16[80,2048]{1,0:T(8,128)(2,1)} %param.8), channel_id=1, source_target_pairs={{0,1},{1,2},{2,3},{3,4},{4,5},{5,6},{6,7},{7,8},{8,9},{9,10},{10,1... | collective-permute-start | bytes 983048 | tf_op jit(solution)/shard_map/ppermute | solution.py:57
  10.6 11.6 %collective-permute-start.1 = (bf16[80,2048]{1,0:T(8,128)(2,1)}, bf16[80,2048]{1,0:T(8,128)(2,1)S(1)}, u32[]{:S(2)}, u32[]{:S(2)}) collective-permute-start(bf16[80,2048]{1,0:T(8,128)(2,1)} %param.8), channel_id=1, source_target_pairs={{0,15},{1,0},{2,1},{3,2},{4,3},{5,4},{6,5},{7,6},{8,7},{9,8},{10,9... | collective-permute-start | bytes 983048 | tf_op jit(solution)/shard_map/ppermute | solution.py:60
  19.5 90.2 %copy-start.3 = (bf16[128,768]{1,0:T(8,128)(2,1)S(1)}, bf16[128,768]{1,0:T(8,128)(2,1)}, u32[]{:S(2)}) copy-start(bf16[128,768]{1,0:T(8,128)(2,1)} %param.10) | copy-start | bytes 589828
  20.3 11.1 %collective-permute-start.2 = (bf16[80,2048]{1,0:T(8,128)(2,1)S(1)}, bf16[80,2048]{1,0:T(8,128)(2,1)S(1)}, u32[]{:S(2)}, u32[]{:S(2)}) collective-permute-start(bf16[80,2048]{1,0:T(8,128)(2,1)S(1)} %collective-permute-done), channel_id=1, source_target_pairs={{0,1},{1,2},{2,3},{3,4},{4,5},{5,6},{6,7},{7,8},{8,9},{9,10},{10,1... | collective-permute-start | bytes 983048 | tf_op jit(solution)/shard_map/ppermute | solution.py:57
  22.2 11.1 %collective-permute-start.3 = (bf16[80,2048]{1,0:T(8,128)(2,1)S(1)}, bf16[80,2048]{1,0:T(8,128)(2,1)S(1)}, u32[]{:S(2)}, u32[]{:S(2)}) collective-permute-start(bf16[80,2048]{1,0:T(8,128)(2,1)S(1)} %collective-permute-done.1), channel_id=1, source_target_pairs={{0,15},{1,0},{2,1},{3,2},{4,3},{5,4},{6,5},{7,6},{8,7},{9,8},{10,9... | collective-permute-start | bytes 983048 | tf_op jit(solution)/shard_map/ppermute | solution.py:60
  31.4 11.1 %collective-permute-start.4 = (bf16[80,2048]{1,0:T(8,128)(2,1)S(1)}, bf16[80,2048]{1,0:T(8,128)(2,1)S(1)}, u32[]{:S(2)}, u32[]{:S(2)}) collective-permute-start(bf16[80,2048]{1,0:T(8,128)(2,1)S(1)} %collective-permute-done.2), channel_id=1, source_target_pairs={{0,1},{1,2},{2,3},{3,4},{4,5},{5,6},{6,7},{7,8},{8,9},{9,10},{10,1... | collective-permute-start | bytes 983048 | tf_op jit(solution)/shard_map/ppermute | solution.py:57
  33.3 11.1 %collective-permute-start.5 = (bf16[80,2048]{1,0:T(8,128)(2,1)S(1)}, bf16[80,2048]{1,0:T(8,128)(2,1)S(1)}, u32[]{:S(2)}, u32[]{:S(2)}) collective-permute-start(bf16[80,2048]{1,0:T(8,128)(2,1)S(1)} %collective-permute-done.3), channel_id=1, source_target_pairs={{0,15},{1,0},{2,1},{3,2},{4,3},{5,4},{6,5},{7,6},{8,7},{9,8},{10,9... | collective-permute-start | bytes 983048 | tf_op jit(solution)/shard_map/ppermute | solution.py:60
  42.5 11.6 %collective-permute-start.6 = (bf16[80,2048]{1,0:T(8,128)(2,1)S(1)}, bf16[80,2048]{1,0:T(8,128)(2,1)S(1)}, u32[]{:S(2)}, u32[]{:S(2)}) collective-permute-start(bf16[80,2048]{1,0:T(8,128)(2,1)S(1)} %collective-permute-done.4), channel_id=1, source_target_pairs={{0,1},{1,2},{2,3},{3,4},{4,5},{5,6},{6,7},{7,8},{8,9},{9,10},{10,1... | collective-permute-start | bytes 983048 | tf_op jit(solution)/shard_map/ppermute | solution.py:57
  44.4 11.6 %collective-permute-start.7 = (bf16[80,2048]{1,0:T(8,128)(2,1)S(1)}, bf16[80,2048]{1,0:T(8,128)(2,1)S(1)}, u32[]{:S(2)}, u32[]{:S(2)}) collective-permute-start(bf16[80,2048]{1,0:T(8,128)(2,1)S(1)} %collective-permute-done.5), channel_id=1, source_target_pairs={{0,15},{1,0},{2,1},{3,2},{4,3},{5,4},{6,5},{7,6},{8,7},{9,8},{10,9... | collective-permute-start | bytes 983048 | tf_op jit(solution)/shard_map/ppermute | solution.py:60
  54.1 12.7 %collective-permute-start.8 = (bf16[80,2048]{1,0:T(8,128)(2,1)S(1)}, bf16[80,2048]{1,0:T(8,128)(2,1)S(1)}, u32[]{:S(2)}, u32[]{:S(2)}) collective-permute-start(bf16[80,2048]{1,0:T(8,128)(2,1)S(1)} %collective-permute-done.6), channel_id=1, source_target_pairs={{0,1},{1,2},{2,3},{3,4},{4,5},{5,6},{6,7},{7,8},{8,9},{9,10},{10,1... | collective-permute-start | bytes 983048 | tf_op jit(solution)/shard_map/ppermute | solution.py:57
  56.0 12.8 %collective-permute-start.9 = (bf16[80,2048]{1,0:T(8,128)(2,1)S(1)}, bf16[80,2048]{1,0:T(8,128)(2,1)S(1)}, u32[]{:S(2)}, u32[]{:S(2)}) collective-permute-start(bf16[80,2048]{1,0:T(8,128)(2,1)S(1)} %collective-permute-done.7), channel_id=1, source_target_pairs={{0,15},{1,0},{2,1},{3,2},{4,3},{5,4},{6,5},{7,6},{8,7},{9,8},{10,9... | collective-permute-start | bytes 983048 | tf_op jit(solution)/shard_map/ppermute | solution.py:60
  66.7 13.7 %collective-permute-start.10 = (bf16[80,2048]{1,0:T(8,128)(2,1)S(1)}, bf16[80,2048]{1,0:T(8,128)(2,1)S(1)}, u32[]{:S(2)}, u32[]{:S(2)}) collective-permute-start(bf16[80,2048]{1,0:T(8,128)(2,1)S(1)} %collective-permute-done.8), channel_id=1, source_target_pairs={{0,1},{1,2},{2,3},{3,4},{4,5},{5,6},{6,7},{7,8},{8,9},{9,10},{10,1... | collective-permute-start | bytes 983048 | tf_op jit(solution)/shard_map/ppermute | solution.py:57
  68.8 14.0 %collective-permute-start.11 = (bf16[80,2048]{1,0:T(8,128)(2,1)S(1)}, bf16[80,2048]{1,0:T(8,128)(2,1)S(1)}, u32[]{:S(2)}, u32[]{:S(2)}) collective-permute-start(bf16[80,2048]{1,0:T(8,128)(2,1)S(1)} %collective-permute-done.9), channel_id=1, source_target_pairs={{0,15},{1,0},{2,1},{3,2},{4,3},{5,4},{6,5},{7,6},{8,7},{9,8},{10,9... | collective-permute-start | bytes 983048 | tf_op jit(solution)/shard_map/ppermute | solution.py:60
  80.5 14.7 %collective-permute-start.12 = (bf16[80,2048]{1,0:T(8,128)(2,1)S(1)}, bf16[80,2048]{1,0:T(8,128)(2,1)S(1)}, u32[]{:S(2)}, u32[]{:S(2)}) collective-permute-start(bf16[80,2048]{1,0:T(8,128)(2,1)S(1)} %collective-permute-done.10), channel_id=1, source_target_pairs={{0,1},{1,2},{2,3},{3,4},{4,5},{5,6},{6,7},{7,8},{8,9},{9,10},{10,1... | collective-permute-start | bytes 983048 | tf_op jit(solution)/shard_map/ppermute | solution.py:57
  82.8 15.0 %collective-permute-start.13 = (bf16[80,2048]{1,0:T(8,128)(2,1)S(1)}, bf16[80,2048]{1,0:T(8,128)(2,1)S(1)}, u32[]{:S(2)}, u32[]{:S(2)}) collective-permute-start(bf16[80,2048]{1,0:T(8,128)(2,1)S(1)} %collective-permute-done.11), channel_id=1, source_target_pairs={{0,15},{1,0},{2,1},{3,2},{4,3},{5,4},{6,5},{7,6},{8,7},{9,8},{10,9... | collective-permute-start | bytes 983048 | tf_op jit(solution)/shard_map/ppermute | solution.py:60
  95.2 13.8 %collective-permute-start.14 = (bf16[80,2048]{1,0:T(8,128)(2,1)S(1)}, bf16[80,2048]{1,0:T(8,128)(2,1)S(1)}, u32[]{:S(2)}, u32[]{:S(2)}) collective-permute-start(bf16[80,2048]{1,0:T(8,128)(2,1)S(1)} %collective-permute-done.12), channel_id=1, source_target_pairs={{0,1},{1,2},{2,3},{3,4},{4,5},{5,6},{6,7},{7,8},{8,9},{9,10},{10,1... | collective-permute-start | bytes 983048 | tf_op jit(solution)/shard_map/ppermute | solution.py:57
  109.7 147.4 %copy-start.2 = (bf16[1,128,768]{2,1,0:T(8,128)(2,1)S(1)}, bf16[1,128,768]{2,1,0:T(8,128)(2,1)}, u32[]{:S(2)}) copy-start(bf16[1,128,768]{2,1,0:T(8,128)(2,1)} %param.11) | copy-start | bytes 589828
  109.7 148.3 %copy-start.4 = (s32[1,128]{1,0:T(1,128)S(1)}, s32[1,128]{1,0:T(1,128)}, u32[]{:S(2)}) copy-start(s32[1,128]{1,0:T(1,128)} %param.15) | copy-start | bytes 1540
  109.7 219.1 %copy-start.5 = (s32[1,128]{1,0:T(1,128)S(1)}, s32[1,128]{1,0:T(1,128)}, u32[]{:S(2)}) copy-start(s32[1,128]{1,0:T(1,128)} %param.14) | copy-start | bytes 1540
  116.4 212.4 %all-gather.2.cloned.1.call-start = ((), (), s32[]{:S(2)}) async-start(), calls=%async_computation.5 | async-start | bytes 4177920 | tf_op jit(solution)/shard_map/all_gather | solution.py:91
  253.2 15.8 %all-to-all-start = ((s32[32,5,1]{1,2,0:T(1,128)}), s32[32,5,1]{1,2,0:T(1,128)S(1)}, u32[]{:S(2)}, u32[]{:S(2)}) async-start(s32[32,5,1]{1,2,0:T(1,128)} %bitcast.5), calls=%async_computation | async-start | bytes 32768 | tf_op jit(solution)/shard_map/all_to_all | solution.py:88
  389.1 44.0 %all-to-all-start.2 = ((f32[32,5,1]{1,2,0:T(1,128)}), f32[32,5,1]{1,2,0:T(1,128)S(1)}, u32[]{:S(2)}, u32[]{:S(2)}) async-start(f32[32,5,1]{1,2,0:T(1,128)} %bitcast.9), calls=%async_computation.3 | async-start | bytes 32768 | tf_op jit(solution)/shard_map/all_to_all | solution.py:97
Sparse Core Ops, SparseCore 0:
  116.6 89.3 reduce-scatter.1
  251.7 55.0 all-gather.1
